TPU v7x, 128 devices: a whole 4x4x4 slice. The times are simulated.
128 devices in a mesh: leaf: 4 (over y), row: 8 (over z, core), col: 4 (over x).
Axes of the slice: x: 4, y: 4, z: 4, core: 2. Of those that a mesh axis runs over, the one named last changes fastest.
Arguments:
- sigma_top: float32 [1024, 1024], P(('leaf', 'row'), 'col')
- panels: float32 [4, 7, 1024, 512], P('leaf', None, 'row', 'col'), may hold values from -0.1875 to 0.1875
- inverse_diag: float32 [4, 7, 512, 512], P('leaf', None, 'col')
- slot_lists: int32 [4, 6, 8], P('leaf'), may hold values from -1 to 11, as said below
- parent_links: int32 [4, 4], P('leaf'), may hold values from 1 to 2
Outputs:
- ancestor_block: float32 [4, 7, 1024, 512], P('leaf', None, 'row', 'col')
- diagonal_block: float32 [4, 7, 512, 512], P('leaf', None, None, 'col')
Inputs may be any that keep to these rules, and one draw needn't show every extreme that they name: `slot_lists`: in every row, entries 0 to 3 are 8 to 11 in order (the parent's own tiles); then come 1 to 3 distinct parent ancestor slots, below 8 for supernodes 1 and 2 and below 4 for supernodes 3 to 6; the rest are -1, so every row has padding. `parent_links`: each supernode 3 to 6 has supernode 1 or 2 as its parent. `sigma_top`: symmetric.
All inputs are finite; a program needn't handle non-finite values.
Results may differ from a plain program's by a relative error of at most 0.0001.
Values sent between devices are 32-bit elements; how exact they have to be, the bound alone decides.
A program may use at most 128 MiB of HBM per device.

v0:
```python
import jax
import jax.numpy as jnp
from jax import lax
from jax.sharding import PartitionSpec as P

TILE = 128
HIGHEST = lax.Precision.HIGHEST


def mm(a, b):
    return jnp.matmul(a, b, precision=HIGHEST, preferred_element_type=jnp.float32)


def tile_rows(matrix, index, tile):
    return lax.dynamic_slice_in_dim(matrix, index * tile, tile, 0)


def tile_cols(matrix, index, tile):
    return lax.dynamic_slice_in_dim(matrix, index * tile, tile, 1)


def scatter_factor(factor_col, slots, positions, tile):
    tiles = factor_col.reshape(slots.shape[0], tile, factor_col.shape[1])
    hits = slots[:, None] == jnp.arange(positions, dtype=slots.dtype)[None, :]
    present = jnp.any(hits, axis=0)
    source = jnp.argmax(hits, axis=0)
    moved = jnp.take(tiles, source, axis=0)
    moved = jnp.where(present[:, None, None], moved, 0.0)
    return moved.reshape(positions * tile, factor_col.shape[1])


def body(sigma_top, panels, inverse_diag, slot_lists, parent_links):
    tile = TILE
    row_count = lax.axis_size("row")
    col_count = lax.axis_size("col")
    leaf_count = lax.axis_size("leaf")
    r = lax.axis_index("row")
    c = lax.axis_index("col")
    panel = panels[0]
    inverse = inverse_diag[0]
    picks_all = slot_lists[0]
    parents = parent_links[0]
    nodes = panel.shape[0]
    width = inverse.shape[2]
    own_tiles = width // tile
    slot_count = picks_all.shape[1]
    positions = slot_count + own_tiles
    band = width // row_count
    partial_factor = mm(panel, inverse)
    factor_rows = lax.psum(partial_factor, "col")
    living = jnp.concatenate([jnp.ones((1, slot_count), jnp.bool_), picks_all >= 0], axis=0)
    live_here = jnp.take(living, r, axis=1).astype(jnp.float32)
    factor_rows = factor_rows * live_here[:, None, None]
    factor_tile = lax.dynamic_slice_in_dim(factor_rows, c * tile, tile, 2)
    factor_cols = lax.all_gather(factor_tile, "row", axis=1, tiled=True)
    inverse_band = lax.dynamic_slice_in_dim(inverse, r * band, band, 2)
    partial_gram = mm(jnp.transpose(inverse_band, (0, 2, 1)), inverse)
    gram_piece = lax.psum_scatter(partial_gram, "col", scatter_dimension=2, tiled=True)
    local_rows, local_cols = sigma_top.shape
    gathered = lax.all_gather(sigma_top, ("leaf", "row", "col"), axis=0)
    sigma = gathered.reshape(leaf_count * row_count, col_count, local_rows, local_cols)
    sigma = jnp.transpose(sigma, (0, 2, 1, 3)).reshape(
        leaf_count * row_count * local_rows, col_count * local_cols
    )

    def diag_partial(first, products):
        rows = factor_rows[first : first + products.shape[0]]
        return mm(jnp.transpose(rows, (0, 2, 1)), products)

    def reduce_and_gather(first, products):
        count = products.shape[0]
        piece = lax.psum_scatter(
            diag_partial(first, products), "row", scatter_dimension=1, tiled=True
        )
        piece = piece + gram_piece[first : first + count]
        both = jnp.concatenate([products, piece], axis=1)
        everything = lax.all_gather(both, ("row", "col"), axis=0)
        return everything.reshape(row_count, col_count, count, tile + band, tile)

    bands_per_tile = tile // band

    def product_col_t(gathered, node, m):
        tiles = lax.dynamic_index_in_dim(gathered[:, :, :, :tile], m, 1, keepdims=False)
        tiles = lax.dynamic_index_in_dim(tiles, node, 1, keepdims=False)
        return jnp.transpose(tiles, (2, 0, 1)).reshape(tile, -1)

    def product_row(gathered, node, q):
        tiles = lax.dynamic_index_in_dim(gathered[:, :, :, :tile], q, 0, keepdims=False)
        tiles = lax.dynamic_index_in_dim(tiles, node, 1, keepdims=False)
        return jnp.transpose(tiles, (1, 0, 2)).reshape(tile, -1)

    def diag_row(gathered, node, m):
        pieces = lax.dynamic_slice_in_dim(
            gathered[:, :, :, tile:], m * bands_per_tile, bands_per_tile, 0
        )
        pieces = lax.dynamic_index_in_dim(pieces, node, 2, keepdims=False)
        return jnp.transpose(pieces, (0, 2, 1, 3)).reshape(tile, -1)

    def diag_col(gathered, m):
        pieces = lax.dynamic_index_in_dim(gathered[:, :, :, tile:], m, 1, keepdims=False)
        return jnp.transpose(pieces, (1, 0, 2, 3)).reshape(pieces.shape[1], -1, tile)

    own_row = jnp.minimum(r, own_tiles - 1)
    upper = r < own_tiles
    product_0 = mm(tile_rows(sigma, r, tile), factor_cols[0])
    gathered_0 = reduce_and_gather(0, product_0[None])
    top_row_1 = jnp.concatenate(
        [-product_col_t(gathered_0, 0, own_row), diag_row(gathered_0, 0, own_row)], axis=1
    )
    level_1 = []
    for node in (1, 2):
        slots = picks_all[node - 1]
        spread = scatter_factor(factor_cols[node], slots, positions, tile)
        source = slots[jnp.maximum(r, own_tiles)]
        source_row = jnp.maximum(source, 0)
        low_row = jnp.concatenate(
            [tile_rows(sigma, source_row, tile), -product_row(gathered_0, 0, source_row)], axis=1
        )
        low_row = jnp.where(source >= 0, low_row, 0.0)
        row = jnp.where(upper, top_row_1, low_row)
        level_1.append(mm(row, spread))
    product_1 = jnp.stack(level_1)
    gathered_1 = reduce_and_gather(1, product_1)
    level_2 = []
    for node in range(3, nodes):
        slots = picks_all[node - 1]
        parent = parents[node - 3] - 1
        parent_slots = jnp.take(picks_all, parent, axis=0)
        spread = scatter_factor(factor_cols[node], slots, positions, tile)
        top_row = jnp.concatenate(
            [-product_col_t(gathered_1, parent, own_row), diag_row(gathered_1, parent, own_row)],
            axis=1,
        )
        source = slots[jnp.maximum(r, own_tiles)]
        source_row = jnp.clip(source, 0, own_tiles - 1)
        corner_tiles = product_col_t(gathered_0, 0, source_row).reshape(tile, slot_count, tile)
        corner_picks = parent_slots[own_tiles:]
        corner = jnp.take(corner_tiles, jnp.maximum(corner_picks, 0), axis=1)
        corner = jnp.where((corner_picks >= 0)[None, :, None], -corner, 0.0).reshape(tile, -1)
        low_row = jnp.concatenate(
            [
                diag_row(gathered_0, 0, source_row),
                corner,
                -product_row(gathered_1, parent, source_row),
            ],
            axis=1,
        )
        low_row = jnp.where(source >= 0, low_row, 0.0)
        row = jnp.where(upper, top_row, low_row)
        level_2.append(mm(row, spread))
    product_2 = jnp.stack(level_2)
    first_2 = 3
    count_2 = product_2.shape[0]
    gram_rows = jnp.zeros((count_2, width, tile), jnp.float32)
    gram_rows = lax.dynamic_update_slice_in_dim(
        gram_rows, gram_piece[first_2 : first_2 + count_2], r * band, 1
    )
    diag_2 = lax.psum(diag_partial(first_2, product_2) + gram_rows, "row")
    products = jnp.concatenate([product_0[None], product_1, product_2], axis=0)
    diag_cols = jnp.concatenate([diag_col(gathered_0, c), diag_col(gathered_1, c), diag_2], axis=0)
    return ((-products)[None], diag_cols[None])


def solution(mesh):
    return jax.shard_map(
        body,
        mesh=mesh,
        in_specs=(
            P(("leaf", "row"), "col"),
            P("leaf", None, "row", "col"),
            P("leaf", None, "col", None),
            P("leaf", None, None),
            P("leaf", None),
        ),
        out_specs=(P("leaf", None, "row", "col"), P("leaf", None, None, "col")),
        check_vma=False,
    )
```

profile of v0, /device:TPU:0, one launch (start us, length us, event | category | flops | bytes accessed | tf_op | source)
XLA Modules:
  0.0 443.9 jit_solution(9169907735359701775)
XLA Ops:
  9.5 3.9 fusion.2
  14.3 57.6 %all-reduce.4.cloned.1.call-done = f32[7,128,512]{2,1,0:T(8,128)} async-done(((f32[7,128,512]{2,1,0:T(8,128)}), f32[7,128,512]{2,1,0:T(8,128)}) %all-reduce.4.cloned.1.call-update) | async-done | bytes 1835024 | tf_op jit(solution)/shard_map/psum | solution.py:50
  75.9 2.3 fusion
  78.3 18.1 %all-gather.10.cloned.1.call-done = f32[4096,256]{1,0:T(8,128)} async-done(((f32[32,256]{1,0:T(8,128)}), f32[4096,256]{1,0:T(8,128)}) %all-gather.10.cloned.1.call-update) | async-done | bytes 4194320 | tf_op jit(solution)/shard_map/all_gather | solution.py:60
  96.3 5.8 %copy.183 = f32[32,4,32,256]{3,1,2,0:T(4,128)S(1)} copy(f32[32,4,32,256]{3,2,1,0:T(8,128)} %bitcast.299) | data formatting | bytes 8388608 | tf_op jit(solution)/shard_map/reshape | solution.py:61
  102.2 3.0 copy.234
  105.1 20.2 %all-gather.8.cloned.1.call-done = f32[7,1024,128]{2,1,0:T(8,128)} async-done(((f32[7,128,128]{2,1,0:T(8,128)}), f32[7,1024,128]{2,1,0:T(8,128)}) %all-gather.8.cloned.1.call-update) | async-done | bytes 3670032 | tf_op jit(solution)/shard_map/all_gather | solution.py:55
  125.3 2.5 bitcast_dynamic-update-slice_fusion.6
  129.2 30.5 %reduce-scatter.4.cloned.1.call-done = f32[1,64,128]{2,1,0:T(8,128)} async-done(((f32[1,512,128]{2,1,0:T(8,128)}), f32[1,64,128]{2,1,0:T(8,128)}) %reduce-scatter.4.cloned.1.call-update) | async-done | bytes 32784 | tf_op jit(solution)/shard_map/reduce_scatter | solution.py:72
  170.7 3.1 fusion.109
  173.7 2.5 gather_fusion.1
  177.7 2.3 select_select_fusion.4
  181.0 2.3 constant_dynamic-slice_fusion.14
  183.3 22.6 %all-gather.12.cloned.1.call-done = f32[32,192,128]{2,1,0:T(8,128)} async-done(((f32[1,192,128]{2,1,0:T(8,128)}), f32[32,192,128]{2,1,0:T(8,128)}) %all-gather.12.cloned.1.call-update) | async-done | bytes 3145744 | tf_op jit(solution)/shard_map/all_gather | solution.py:77
  207.3 2.1 slice.193
  216.4 3.2 constant_dynamic-slice_fusion.6
  220.9 3.1 bitcast_dynamic-update-slice_fusion.5
  227.5 30.5 %reduce-scatter.8.cloned.1.call-done = f32[2,64,128]{2,1,0:T(8,128)} async-done(((f32[2,512,128]{2,1,0:T(8,128)}), f32[2,64,128]{2,1,0:T(8,128)}) %reduce-scatter.8.cloned.1.call-update) | async-done | bytes 65552 | tf_op jit(solution)/shard_map/reduce_scatter | solution.py:72
  273.0 2.5 gather_fusion.7
  289.5 2.3 gather_fusion.8
  299.2 2.3 gather_fusion.6
  306.9 2.1 copy.203
  309.0 2.3 gather_fusion.4
  316.7 2.1 copy.195
  318.8 2.3 gather_fusion.2
  328.1 3.2 slice.198
  336.7 2.1 copy.232
  338.8 2.1 copy.231
  340.9 2.2 negate_bitcast_fusion
  361.5 3.3 bitcast_dynamic-update-slice_fusion.3
  375.5 58.1 %all-reduce.6.cloned.1.call-done = f32[4,512,128]{2,1,0:T(8,128)} async-done(((f32[4,512,128]{2,1,0:T(8,128)}), f32[4,512,128]{2,1,0:T(8,128)}) %all-reduce.6.cloned.1.call-update) | async-done | bytes 1048592 | tf_op jit(solution)/shard_map/psum | solution.py:158
  433.6 2.7 maximum_bitcast_fusion
  (223 shorter events, 109.3 us)
Async XLA Ops:
  8.0 63.9 %all-reduce.4.cloned.1.call-start = ((), (), s32[]{:S(2)}) async-start(), calls=%async_computation.3 | async-start | bytes 3670016 | tf_op jit(solution)/shard_map/psum | solution.py:50
  13.4 82.9 %all-gather.10.cloned.1.call-start = ((), (), s32[]{:S(2)}) async-start(), calls=%async_computation.9 | async-start | bytes 4227072 | tf_op jit(solution)/shard_map/all_gather | solution.py:60
  14.0 111.3 %all-gather.8.cloned.1.call-start = ((), (), s32[]{:S(2)}) async-start(), calls=%async_computation.4 | async-start | bytes 4128768 | tf_op jit(solution)/shard_map/all_gather | solution.py:55
  75.8 53.4 %reduce-scatter.6.cloned.1.call-start = ((), (), s32[]{:S(2)}) async-start(), calls=%async_computation.6 | async-start | bytes 1146880 | tf_op jit(solution)/shard_map/reduce_scatter | solution.py:58
  78.2 81.5 %reduce-scatter.4.cloned.1.call-start = ((), (), s32[]{:S(2)}) async-start(), calls=%async_computation.5 | async-start | bytes 294912 | tf_op jit(solution)/shard_map/reduce_scatter | solution.py:72
  102.1 25.6 %copy-start.3 = (f32[7,128,512]{2,1,0:T(8,128)S(1)}, f32[7,128,512]{2,1,0:T(8,128)}, u32[]{:S(2)}) copy-start(f32[7,128,512]{2,1,0:T(8,128)} %copy-done.2) | copy-start | bytes 5505028
  129.1 76.9 %all-gather.12.cloned.1.call-start = ((), (), s32[]{:S(2)}) async-start(), calls=%async_computation.10 | async-start | bytes 3244032 | tf_op jit(solution)/shard_map/all_gather | solution.py:77
  161.2 96.9 %reduce-scatter.8.cloned.1.call-start = ((), (), s32[]{:S(2)}) async-start(), calls=%async_computation.7 | async-start | bytes 589824 | tf_op jit(solution)/shard_map/reduce_scatter | solution.py:72
  177.7 2.3 copy-start.13
  207.3 2.1 copy-start.7
  220.9 3.2 copy-start.15
  220.9 3.2 copy-start.16
  220.9 3.2 copy-start.20
  220.9 3.2 copy-start.36
  225.7 34.1 %copy-start.41 = (s32[1,4]{1,0:T(1,128)S(1)}, s32[1,4]{1,0:T(1,128)}, u32[]{:S(2)}) copy-start(s32[1,4]{1,0:T(1,128)} %param.15) | copy-start | bytes 52
  227.5 48.1 %copy-start.9 = (f32[1,1024,128]{2,1,0:T(8,128)S(1)}, f32[1,1024,128]{2,1,0:T(8,128)}, u32[]{:S(2)}) copy-start(f32[1,1024,128]{2,1,0:T(8,128)} %get-tuple-element.49) | copy-start | bytes 1572868
  227.5 98.9 %all-gather.14.cloned.1.call-start = ((), (), s32[]{:S(2)}) async-start(), calls=%async_computation.11 | async-start | bytes 6488064 | tf_op jit(solution)/shard_map/all_gather | solution.py:77
  259.7 173.9 %all-reduce.6.cloned.1.call-start = ((), (), s32[]{:S(2)}) async-start(), calls=%async_computation.8 | async-start | bytes 2097152 | tf_op jit(solution)/shard_map/psum | solution.py:158
  281.6 2.2 copy-start.24
  281.7 3.1 copy-start.23
  282.8 2.9 copy-start.22
  283.8 2.7 copy-start.21
  328.1 3.2 copy-start.8
  331.4 4.0 copy-start.5
  361.4 3.4 copy-start.14
  361.4 3.4 copy-start.19
  361.5 3.4 copy-start.28
  361.5 3.4 copy-start.30
  361.5 3.4 copy-start.33
  361.5 3.4 copy-start.37
  371.5 3.1 copy-start.38
  433.6 2.7 copy-start.1
  (19 other events, 29.3 us)
Sparse Core Ops, SparseCore 0:
  13.5 58.3 all-reduce.3
  79.1 22.6 reduce-scatter.5
  129.2 30.4 reduce-scatter.3
  162.1 43.8 all-gather.11
  227.6 30.4 reduce-scatter.7
  260.2 47.9 all-gather.13
Sparse Core Ops, SparseCore 1:
  17.0 79.3 all-gather.9
  98.5 26.8 all-gather.7
  372.6 60.9 all-reduce.5
where the time goes:
time: 446 us; the launch traced here: 444 us
  waiting for transfers between devices  238 us (53%)
  local copies, waits for them, and re-layouts  110 us (25%)
  other arithmetic  38.9 us (9%)
  between operations  29.3 us (7%)
  matrix products  26.3 us (6%)
    reduce_scatter x2, waiting for transfers between devices, reduce_and_gather(): lax.psum_scatter(diag_partial(first, products), 'row', scatter_dimension=...  61.1 us
    psum x1, waiting for transfers between devices, body(): diag_2 = lax.psum(diag_partial(first_2, product_2) + gram_rows, 'row')  58.1 us
    psum x1, waiting for transfers between devices, body(): factor_rows = lax.psum(partial_factor, 'col')  57.6 us
    dot_general x12, matrix products, mm(): jnp.matmul(a, b, precision=HIGHEST, preferred_element_type=jnp.float32)  26.3 us
    all_gather x2, waiting for transfers between devices, reduce_and_gather(): everything = lax.all_gather(both, ('row', 'col'), axis=0)  22.6 us
    all_gather x1, waiting for transfers between devices, body(): factor_cols = lax.all_gather(factor_tile, 'row', axis=1, tiled=True)  20.2 us
    all_gather x1, waiting for transfers between devices, body(): gathered = lax.all_gather(sigma_top, ('leaf', 'row', 'col'), axis=0)  18.1 us
    neg x8, local copies, waits for them, and re-layouts, body(): -product_row(gathered_1, parent, source_row)  14.3 us
  transfers between devices with their start and end apart: 9, of which 7 were waited for; matrix products, arithmetic and copies ran while one was open for 22% of the time, Pallas kernels for 0%

commit v1 on v0

--- a/solution.py
+++ b/solution.py
@@ -47,7 +47,7 @@
     positions = slot_count + own_tiles
     band = width // row_count
     partial_factor = mm(panel, inverse)
-    factor_rows = lax.psum(partial_factor, "col")
+    factor_rows = jnp.sum(lax.all_gather(partial_factor, "col"), axis=0)
     living = jnp.concatenate([jnp.ones((1, slot_count), jnp.bool_), picks_all >= 0], axis=0)
     live_here = jnp.take(living, r, axis=1).astype(jnp.float32)
     factor_rows = factor_rows * live_here[:, None, None]

time: 446 us -> 539 us (1.21)
  waiting for transfers between devices: 238 us -> 327 us
    all_gather x0 -> x1, waiting for transfers between devices: none -> 75.9 us  [body(): factor_rows = jnp.sum(lax.all_gather(partial_factor, 'col'), axis=0)]
    psum x1 -> x0, waiting for transfers between devices: 57.6 us -> none  [body(): factor_rows = lax.psum(partial_factor, 'col')]
    all_gather x1, waiting for transfers between devices: 18.1 us -> 56.6 us  [body(): gathered = lax.all_gather(sigma_top, ('leaf', 'row', 'col'), axis=0)]
    reduce_scatter x1, waiting for transfers between devices: 0.02 us -> 22.6 us  [body(): lax.psum_scatter(partial_gram, 'col', scatter_dimension=2, tiled=True)]
    reduce_sum x0 -> x1, other arithmetic: none -> 5.41 us  [body(): factor_rows = jnp.sum(lax.all_gather(partial_factor, 'col'), axis=0)]
  transfers between devices with their start and end apart: 9 -> 9, of which waited for: 7 -> 8; matrix products, arithmetic and copies ran while one was open for 22% -> 20% of each run, Pallas kernels for 0% -> 0%
where the time goes in v1:
time: 539 us; the launch traced here: 536 us
  waiting for transfers between devices  327 us (61%)
  local copies, waits for them, and re-layouts  113 us (21%)
  other arithmetic  44 us (8%)
  between operations  27 us (5%)
  matrix products  24.6 us (5%)
    all_gather x1, waiting for transfers between devices, body(): factor_rows = jnp.sum(lax.all_gather(partial_factor, 'col'), axis=0)  75.9 us
    reduce_scatter x2, waiting for transfers between devices, reduce_and_gather(): lax.psum_scatter(diag_partial(first, products), 'row', scatter_dimension=...  63.8 us
    psum x1, waiting for transfers between devices, body(): diag_2 = lax.psum(diag_partial(first_2, product_2) + gram_rows, 'row')  58.6 us
    all_gather x1, waiting for transfers between devices, body(): gathered = lax.all_gather(sigma_top, ('leaf', 'row', 'col'), axis=0)  56.6 us
    all_gather x1, waiting for transfers between devices, body(): factor_cols = lax.all_gather(factor_tile, 'row', axis=1, tiled=True)  25 us
    dot_general x12, matrix products, mm(): jnp.matmul(a, b, precision=HIGHEST, preferred_element_type=jnp.float32)  24.6 us
    all_gather x2, waiting for transfers between devices, reduce_and_gather(): everything = lax.all_gather(both, ('row', 'col'), axis=0)  24.2 us
    reduce_scatter x1, waiting for transfers between devices, body(): lax.psum_scatter(partial_gram, 'col', scatter_dimension=2, tiled=True)  22.6 us
  transfers between devices with their start and end apart: 9, of which 8 were waited for; matrix products, arithmetic and copies ran while one was open for 20% of the time, Pallas kernels for 0%

profile of v1, /device:TPU:0, one launch (start us, length us, event | category | flops | bytes accessed | tf_op | source)
XLA Modules:
  0.0 536.3 jit_solution(393394744784764036)
XLA Ops:
  8.7 3.9 fusion.2
  13.7 75.9 %all-gather.14.cloned.1.call-done = f32[28,128,512]{2,1,0:T(8,128)} async-done(((f32[7,128,512]{2,1,0:T(8,128)}), f32[28,128,512]{2,1,0:T(8,128)}) %all-gather.14.cloned.1.call-update) | async-done | bytes 7340048 | tf_op jit(solution)/shard_map/all_gather | solution.py:50
  89.6 5.4 %reduce_sum.9 = f32[7,128,512]{2,1,0:T(8,128)} reduce(f32[4,7,128,512]{3,2,1,0:T(8,128)} %bitcast.298, f32[]{:T(128)} %constant.521.clone.1), dimensions={0}, to_apply=%region_0.0 | reduce | flops 1376256 | bytes 9175044 | tf_op jit(solution)/shard_map/reduce_sum | solution.py:50
  95.0 2.8 copy.204
  101.5 2.2 fusion
  103.8 56.6 %all-gather.12.cloned.1.call-done = f32[4096,256]{1,0:T(8,128)} async-done(((f32[32,256]{1,0:T(8,128)}), f32[4096,256]{1,0:T(8,128)}) %all-gather.12.cloned.1.call-update) | async-done | bytes 4194320 | tf_op jit(solution)/shard_map/all_gather | solution.py:60
  160.4 5.8 %copy.203 = f32[32,4,32,256]{3,1,2,0:T(4,128)S(1)} copy(f32[32,4,32,256]{3,2,1,0:T(8,128)} %bitcast.301) | data formatting | bytes 8388608 | tf_op jit(solution)/shard_map/reshape | solution.py:61
  166.2 3.1 copy.263
  169.3 25.0 %all-gather.10.cloned.1.call-done = f32[7,1024,128]{1,2,0:T(8,128)} async-done(((f32[7,128,128]{1,2,0:T(8,128)}), f32[7,1024,128]{1,2,0:T(8,128)}) %all-gather.10.cloned.1.call-update) | async-done | bytes 3670032 | tf_op jit(solution)/shard_map/all_gather | solution.py:55
  194.3 2.4 bitcast_dynamic-update-slice_fusion.6
  197.8 22.6 %reduce-scatter.6.cloned.1.call-done = f32[7,64,128]{2,1,0:T(8,128)} async-done(((f32[7,64,512]{2,1,0:T(8,128)}), f32[7,64,128]{2,1,0:T(8,128)}) %reduce-scatter.6.cloned.1.call-update) | async-done | bytes 229392 | tf_op jit(solution)/shard_map/reduce_scatter | solution.py:58
  220.4 33.3 %reduce-scatter.4.cloned.1.call-done = f32[1,64,128]{2,1,0:T(8,128)} async-done(((f32[1,512,128]{2,1,0:T(8,128)}), f32[1,64,128]{2,1,0:T(8,128)}) %reduce-scatter.4.cloned.1.call-update) | async-done | bytes 32784 | tf_op jit(solution)/shard_map/reduce_scatter | solution.py:72
  264.3 2.3 constant_dynamic-slice_fusion.14
  266.6 3.4 fusion.109
  272.5 2.2 select_select_fusion.4
  275.7 24.2 %all-gather.16.cloned.1.call-done = f32[32,192,128]{2,1,0:T(8,128)} async-done(((f32[1,192,128]{2,1,0:T(8,128)}), f32[32,192,128]{2,1,0:T(8,128)}) %all-gather.16.cloned.1.call-update) | async-done | bytes 3145744 | tf_op jit(solution)/shard_map/all_gather | solution.py:77
  301.2 2.1 slice.193
  308.3 3.3 constant_dynamic-slice_fusion.6
  312.9 3.0 bitcast_dynamic-update-slice_fusion.5
  318.9 30.5 %reduce-scatter.8.cloned.1.call-done = f32[2,64,128]{2,1,0:T(8,128)} async-done(((f32[2,512,128]{2,1,0:T(8,128)}), f32[2,64,128]{2,1,0:T(8,128)}) %reduce-scatter.8.cloned.1.call-update) | async-done | bytes 65552 | tf_op jit(solution)/shard_map/reduce_scatter | solution.py:72
  366.6 2.6 gather_fusion.9
  383.2 2.3 gather_fusion.8
  393.0 2.3 gather_fusion.6
  402.7 2.3 gather_fusion.4
  412.4 2.3 gather_fusion.2
  421.8 3.2 slice.198
  434.5 2.3 negate_bitcast_fusion
  451.1 2.1 copy.256
  453.1 2.1 copy.254
  455.2 3.3 bitcast_dynamic-update-slice_fusion.3
  468.5 58.6 %all-reduce.3.cloned.1.call-done = f32[4,512,128]{2,1,0:T(8,128)} async-done(((f32[4,512,128]{2,1,0:T(8,128)}), f32[4,512,128]{2,1,0:T(8,128)}) %all-reduce.3.cloned.1.call-update) | async-done | bytes 1048592 | tf_op jit(solution)/shard_map/psum | solution.py:158
  527.1 2.7 maximum_bitcast_fusion
  (231 shorter events, 113.4 us)
Async XLA Ops:
  7.2 82.4 %all-gather.14.cloned.1.call-start = ((), (), s32[]{:S(2)}) async-start(), calls=%async_computation.9 | async-start | bytes 9175040 | tf_op jit(solution)/shard_map/all_gather | solution.py:50
  12.6 147.9 %all-gather.12.cloned.1.call-start = ((), (), s32[]{:S(2)}) async-start(), calls=%async_computation.8 | async-start | bytes 4227072 | tf_op jit(solution)/shard_map/all_gather | solution.py:60
  13.3 181.0 %all-gather.10.cloned.1.call-start = ((), (), s32[]{:S(2)}) async-start(), calls=%async_computation.3 | async-start | bytes 4128768 | tf_op jit(solution)/shard_map/all_gather | solution.py:55
  101.5 118.9 %reduce-scatter.6.cloned.1.call-start = ((), (), s32[]{:S(2)}) async-start(), calls=%async_computation.5 | async-start | bytes 1146880 | tf_op jit(solution)/shard_map/reduce_scatter | solution.py:58
  103.8 149.9 %reduce-scatter.4.cloned.1.call-start = ((), (), s32[]{:S(2)}) async-start(), calls=%async_computation.4 | async-start | bytes 294912 | tf_op jit(solution)/shard_map/reduce_scatter | solution.py:72
  166.2 30.5 %copy-start.3 = (f32[7,128,512]{1,2,0:T(8,128)S(1)}, f32[7,128,512]{1,2,0:T(8,128)}, u32[]{:S(2)}) copy-start(f32[7,128,512]{1,2,0:T(8,128)} %copy-done.2) | copy-start | bytes 5505028
  197.8 102.1 %all-gather.16.cloned.1.call-start = ((), (), s32[]{:S(2)}) async-start(), calls=%async_computation.10 | async-start | bytes 3244032 | tf_op jit(solution)/shard_map/all_gather | solution.py:77
  255.1 94.2 %reduce-scatter.8.cloned.1.call-start = ((), (), s32[]{:S(2)}) async-start(), calls=%async_computation.6 | async-start | bytes 589824 | tf_op jit(solution)/shard_map/reduce_scatter | solution.py:72
  301.2 2.1 copy-start.7
  311.5 4.3 copy-start.13
  312.8 3.0 copy-start.20
  312.8 3.0 copy-start.36
  317.4 33.6 %copy-start.41 = (s32[1,4]{1,0:T(1,128)S(1)}, s32[1,4]{1,0:T(1,128)}, u32[]{:S(2)}) copy-start(s32[1,4]{1,0:T(1,128)} %param.15) | copy-start | bytes 52
  317.4 46.5 %copy-start.16 = (f32[1,1024,128]{1,2,0:T(8,128)S(1)}, f32[1,1024,128]{1,2,0:T(8,128)}, u32[]{:S(2)}) copy-start(f32[1,1024,128]{1,2,0:T(8,128)} %get-tuple-element.49) | copy-start | bytes 1572868
  317.4 47.5 %copy-start.15 = (f32[1,1024,128]{1,2,0:T(8,128)S(1)}, f32[1,1024,128]{1,2,0:T(8,128)}, u32[]{:S(2)}) copy-start(f32[1,1024,128]{1,2,0:T(8,128)} %get-tuple-element.50) | copy-start | bytes 1572868
  318.8 46.3 %copy-start.14 = (f32[1,1024,128]{1,2,0:T(8,128)S(1)}, f32[1,1024,128]{1,2,0:T(8,128)}, u32[]{:S(2)}) copy-start(f32[1,1024,128]{1,2,0:T(8,128)} %get-tuple-element.51) | copy-start | bytes 1572868
  318.8 101.2 %all-gather.18.cloned.1.call-start = ((), (), s32[]{:S(2)}) async-start(), calls=%async_computation.11 | async-start | bytes 6488064 | tf_op jit(solution)/shard_map/all_gather | solution.py:77
  350.9 176.1 %all-reduce.3.cloned.1.call-start = ((), (), s32[]{:S(2)}) async-start(), calls=%async_computation.7 | async-start | bytes 2097152 | tf_op jit(solution)/shard_map/psum | solution.py:158
  375.3 2.2 copy-start.24
  375.3 3.1 copy-start.23
  376.5 2.9 copy-start.22
  377.5 2.7 copy-start.21
  421.8 3.2 copy-start.8
  425.1 4.0 copy-start.5
  455.2 3.4 copy-start.12
  455.2 3.4 copy-start.19
  455.2 3.4 copy-start.28
  455.2 3.4 copy-start.30
  455.2 3.4 copy-start.33
  455.2 3.4 copy-start.37
  464.5 3.1 copy-start.38
  527.1 2.7 copy-start.1
  (19 other events, 28.3 us)
Sparse Core Ops, SparseCore 0:
  12.7 76.8 all-gather.13
  92.7 67.6 all-gather.11
  162.7 31.5 all-gather.9
  196.6 23.7 reduce-scatter.5
  223.2 30.4 reduce-scatter.3
  256.0 43.8 all-gather.15
  319.0 30.3 reduce-scatter.7
  351.6 47.9 all-gather.17
  465.6 61.3 all-reduce.2
